TPU v7x, 256 devices: a whole 4x4x8 slice. The times are simulated.
256 devices in a mesh: row: 16 (over z, y_hi), col: 16 (over x, y_lo, core).
Axes of the slice: x: 4, y: 4 (y_hi: 2, y_lo: 2; y = y_hi * 2 + y_lo), z: 8, core: 2. Of those that a mesh axis runs over, the one named last changes fastest.
Arguments:
- tokens: bfloat16 [1024, 14336], P('col', 'row'), may hold values from -6 to 6
- gate_weight: bfloat16 [14336, 26624], P('row', 'col'), may hold values from -0.046875 to 0.046875
- up_weight: bfloat16 [14336, 26624], P('row', 'col'), may hold values from -0.046875 to 0.046875
- upstream: bfloat16 [1024, 26624], P('row', 'col'), may hold values from -0.1875 to 0.1875
Outputs:
- grad_gate: bfloat16 [14336, 26624], P('row', 'col')
- grad_up: bfloat16 [14336, 26624], P('row', 'col')
All inputs are finite; a program needn't handle non-finite values.
Results may differ from a plain program's by a relative error of at most 0.005.
Values may be sent and summed in bfloat16 or wider, within the bound.
A program may use at most 128 MiB of HBM per device.

v0:
```python
import jax
import jax.numpy as jnp
from jax import lax
from jax.sharding import PartitionSpec as P


def swiglu_grads(preacts, cotangent_rows, hidden_cols):
    gate_pre = preacts[:, :hidden_cols]
    up_pre = preacts[:, hidden_cols:]
    squash = jax.nn.sigmoid(gate_pre)
    cotangent = cotangent_rows.astype(jnp.float32)
    d_up = cotangent * gate_pre * squash
    d_gate = cotangent * up_pre * squash * (1.0 + gate_pre * (1.0 - squash))
    return jnp.concatenate([d_gate, d_up], axis=1).astype(jnp.bfloat16)


def local(tokens, gate_weight, up_weight, upstream):
    hidden_cols = gate_weight.shape[1]
    numbers = (((0,), (0,)), ((), ()))
    weights = jnp.concatenate([gate_weight, up_weight], axis=1)
    gathered = lax.all_gather(tokens, "col", axis=0, tiled=True)
    partial_pre = jnp.dot(gathered, weights, preferred_element_type=jnp.float32)
    preacts = lax.psum(partial_pre, "row")
    cotangent_all = lax.all_gather(upstream, "row", axis=0, tiled=True)
    gradients = swiglu_grads(preacts, cotangent_all, hidden_cols)
    weight_grads = lax.dot_general(gathered, gradients, numbers, preferred_element_type=jnp.float32)
    rounded = weight_grads.astype(jnp.bfloat16)
    return (rounded[:, :hidden_cols], rounded[:, hidden_cols:])


def solution(mesh):
    return jax.shard_map(
        local,
        mesh=mesh,
        in_specs=(P("col", "row"), P("row", "col"), P("row", "col"), P("row", "col")),
        out_specs=(P("row", "col"), P("row", "col")),
        check_vma=False,
    )
```

profile of v0, /device:TPU:97, one launch (start us, length us, event | category | flops | bytes accessed | tf_op | source)
XLA Modules:
  0.0 766.3 jit_solution(7752807111683964820)
XLA Ops:
  7.2 0.0 all-gather.5.cloned.1.call-start
  7.2 0.7 all-gather.5.cloned.1.call-update
  7.9 0.0 all-gather.3.cloned.1.call-start
  7.9 0.7 all-gather.3.cloned.1.call-update
  8.6 0.0 all-reduce.2.cloned.1.call-start
  8.7 39.3 %all-gather.5.cloned.1.call-done = bf16[1024,896]{1,0:T(8,128)(2,1)} async-done(((bf16[64,896]{1,0:T(8,128)(2,1)}), bf16[1024,896]{1,0:T(8,128)(2,1)}) %all-gather.5.cloned.1.call-update) | async-done | bytes 1835024 | tf_op jit(solution)/shard_map/all_gather | solution.py:21
  48.0 13.5 %convolution_bitcast_fusion = f32[1024,3328]{0,1:T(8,128)} fusion(bf16[1024,896]{1,0:T(8,128)(2,1)} %all-gather.5.cloned.1.call-done, bf16[896,1664]{1,0:T(8,128)(2,1)} %param.6, bf16[896,1664]{1,0:T(8,128)(2,1)} %param.5), kind=kOutput, calls=%fused_computation | convolution fusion | flops 6118834176 | bytes 21430272 | tf_op jit(solution)/shard_map/dot_general | solution.py:22
  61.5 0.0 all-reduce.2.cloned.1.call-update
  61.5 78.7 %all-gather.3.cloned.1.call-done = bf16[1024,1664]{1,0:T(8,128)(2,1)} async-done(((bf16[64,1664]{1,0:T(8,128)(2,1)}), bf16[1024,1664]{1,0:T(8,128)(2,1)}) %all-gather.3.cloned.1.call-update) | async-done | bytes 3407888 | tf_op jit(solution)/shard_map/all_gather | solution.py:24
  140.3 4.2 copy.9
  144.5 586.7 %all-reduce.2.cloned.1.call-done = f32[1024,3328]{0,1:T(8,128)} async-done(((f32[1024,3328]{0,1:T(8,128)}), f32[1024,3328]{0,1:T(8,128)}) %all-reduce.2.cloned.1.call-update) | async-done | bytes 13631504 | tf_op jit(solution)/shard_map/psum | solution.py:23
  731.2 0.0 copy-start
  731.2 6.7 fusion.2
  737.9 0.0 copy-done
  737.9 10.8 %fusion.8 = bf16[896,3328]{0,1:T(8,128)(2,1)S(1)} fusion(bf16[1024,896]{1,0:T(8,128)(2,1)S(1)} %copy-done, bf16[1024,1664]{0,1:T(8,128)(2,1)S(1)} %get-tuple-element.7, bf16[1024,1664]{0,1:T(8,128)(2,1)S(1)} %get-tuple-element.6), kind=kOutput, calls=%fused_computation.13 | convolution fusion | flops 6123520000 | bytes 14614528 | tf_op jit(solution)/shard_map/dot_general | solution.py:26
  748.8 2.1 fusion.16
  750.8 5.4 copy.10
  756.2 3.5 copy.11
Async XLA Ops:
  7.2 40.8 %all-gather.5.cloned.1.call-start = ((), (), s32[]{:S(2)}) async-start(), calls=%async_computation.1 | async-start | bytes 1949696 | tf_op jit(solution)/shard_map/all_gather | solution.py:21
  7.9 132.4 %all-gather.3.cloned.1.call-start = ((), (), s32[]{:S(2)}) async-start(), calls=%async_computation | async-start | bytes 3620864 | tf_op jit(solution)/shard_map/all_gather | solution.py:24
  8.6 722.5 %all-reduce.2.cloned.1.call-start = ((), (), s32[]{:S(2)}) async-start(), calls=%async_computation.2 | async-start | bytes 27262976 | tf_op jit(solution)/shard_map/psum | solution.py:23
  731.2 6.7 copy-start
Sparse Core Ops, SparseCore 0:
  9.8 38.1 all-gather.4
  50.6 89.6 all-gather.2
  143.0 588.1 all-reduce.1
where the time goes:
time: 767 us; the launch traced here: 766 us
  waiting for transfers between devices  706 us (92%)
  matrix products  24.4 us (3%)
  local copies, waits for them, and re-layouts  15.2 us (2%)
  between operations  13.8 us (2%)
    psum x1, waiting for transfers between devices, local(): preacts = lax.psum(partial_pre, 'row')  587 us
    all_gather x1, waiting for transfers between devices, local(): cotangent_all = lax.all_gather(upstream, 'row', axis=0, tiled=True)  78.7 us
    all_gather x1, waiting for transfers between devices, local(): gathered = lax.all_gather(tokens, 'col', axis=0, tiled=True)  39.3 us
  transfers between devices with their start and end apart: 3, of which 3 were waited for; matrix products, arithmetic and copies ran while one was open for 2% of the time, Pallas kernels for 0%

commit v1 on v0

--- a/solution.py
+++ b/solution.py
@@ -2,6 +2,11 @@
 import jax.numpy as jnp
 from jax import lax
 from jax.sharding import PartitionSpec as P
+
+
+def exchange_gather(array, axis, dim):
+    repeated = jnp.stack([array] * lax.axis_size(axis))
+    return jnp.concatenate(lax.all_to_all(repeated, axis, 0, 0), axis=dim)
 
 
 def swiglu_grads(preacts, cotangent_rows, hidden_cols):
@@ -21,7 +26,7 @@
     gathered = lax.all_gather(tokens, "col", axis=0, tiled=True)
     partial_pre = jnp.dot(gathered, weights, preferred_element_type=jnp.float32)
     preacts = lax.psum(partial_pre, "row")
-    cotangent_all = lax.all_gather(upstream, "row", axis=0, tiled=True)
+    cotangent_all = exchange_gather(upstream, "row", 0)
     gradients = swiglu_grads(preacts, cotangent_all, hidden_cols)
     weight_grads = lax.dot_general(gathered, gradients, numbers, preferred_element_type=jnp.float32)
     rounded = weight_grads.astype(jnp.bfloat16)

time: 767 us -> 719 us (0.937)
  waiting for transfers between devices: 706 us -> 530 us
  blocking collectives: 0 us -> 119 us
    all_to_all x0 -> x1, blocking collectives: none -> 119 us  [exchange_gather(): return jnp.concatenate(lax.all_to_all(repeated, axis, 0, 0), axis=dim)]
    psum x1, waiting for transfers between devices: 587 us -> 489 us  [local(): preacts = lax.psum(partial_pre, 'row')]
    all_gather x1 -> x0, waiting for transfers between devices: 78.7 us -> none  [local(): cotangent_all = lax.all_gather(upstream, 'row', axis=0, tiled=True)]
  transfers between devices with their start and end apart: 3 -> 2, of which waited for: 3 -> 2; matrix products, arithmetic and copies ran while one was open for 2% -> 2% of each run, Pallas kernels for 0% -> 0%
where the time goes in v1:
time: 719 us
  waiting for transfers between devices  530 us (74%)
  blocking collectives  119 us (17%)
  matrix products  24.3 us (3%)
  local copies, waits for them, and re-layouts  19.9 us (3%)
  between operations  14.1 us (2%)
  other arithmetic  12.4 us (2%)
    psum x1, waiting for transfers between devices, local(): preacts = lax.psum(partial_pre, 'row')  489 us
    all_to_all x1, blocking collectives, exchange_gather(): return jnp.concatenate(lax.all_to_all(repeated, axis, 0, 0), axis=dim)  119 us
    all_gather x1, waiting for transfers between devices, local(): gathered = lax.all_gather(tokens, 'col', axis=0, tiled=True)  40.1 us
  transfers between devices with their start and end apart: 2, of which 2 were waited for; matrix products, arithmetic and copies ran while one was open for 2% of the time, Pallas kernels for 0%

profile of v1, /device:TPU:97, one launch (start us, length us, event | category | flops | bytes accessed | tf_op | source)
XLA Modules:
  0.0 719.0 jit_solution(14863140185444737853)
XLA Ops:
  7.2 0.0 all-gather.2.cloned.1.call-start
  7.2 0.7 all-gather.2.cloned.1.call-update
  7.9 0.0 all-reduce.2.cloned.1.call-start
  7.9 40.1 %all-gather.2.cloned.1.call-done = bf16[1024,896]{1,0:T(8,128)(2,1)} async-done(((bf16[64,896]{1,0:T(8,128)(2,1)}), bf16[1024,896]{1,0:T(8,128)(2,1)}) %all-gather.2.cloned.1.call-update) | async-done | bytes 1835024 | tf_op jit(solution)/shard_map/all_gather | solution.py:26
  48.0 13.5 %convolution_bitcast_fusion = f32[1024,3328]{0,1:T(8,128)} fusion(bf16[1024,896]{1,0:T(8,128)(2,1)} %all-gather.2.cloned.1.call-done, bf16[896,1664]{1,0:T(8,128)(2,1)} %param.6, bf16[896,1664]{1,0:T(8,128)(2,1)} %param.5), kind=kOutput, calls=%fused_computation | convolution fusion | flops 6118834176 | bytes 21430272 | tf_op jit(solution)/shard_map/dot_general | solution.py:27
  61.5 0.0 copy-start
  61.5 0.0 all-reduce.2.cloned.1.call-update
  61.6 0.9 copy-done
  62.5 0.4 stack.2
  62.8 118.6 %all_to_all.5 = bf16[16,64,1664]{2,1,0:T(8,128)(2,1)S(1)} all-to-all(bf16[16,64,1664]{2,1,0:T(8,128)(2,1)S(1)} %stack.2), channel_id=1, replica_groups=mesh['row'=16,'col'=16] {'row'}, dimensions={0} | all-to-all | bytes 6815744 | tf_op jit(solution)/shard_map/all_to_all | solution.py:9
  181.4 3.5 bitcast_convert_fusion
  184.9 7.6 %copy.9 = f32[1024,1664]{0,1:T(8,128)} copy(f32[1024,1664]{1,0:T(8,128)} %bitcast_convert_fusion) | data formatting | bytes 13631488 | tf_op jit(solution)/shard_map/convert_element_type | solution.py:16
  192.5 0.0 copy-start.1
  192.5 489.0 %all-reduce.2.cloned.1.call-done = f32[1024,3328]{0,1:T(8,128)} async-done(((f32[1024,3328]{0,1:T(8,128)}), f32[1024,3328]{0,1:T(8,128)}) %all-reduce.2.cloned.1.call-update) | async-done | bytes 13631504 | tf_op jit(solution)/shard_map/psum | solution.py:28
  681.5 8.9 %fusion.2 = (bf16[1024,1664]{0,1:T(8,128)(2,1)S(1)}, bf16[1024,1664]{0,1:T(8,128)(2,1)S(1)}) fusion(f32[1024,1664]{0,1:T(8,128)} %copy.9, f32[1024,3328]{0,1:T(8,128)} %all-reduce.2.cloned.1.call-done), kind=kLoop, calls=%fused_computation.5 | loop fusion | flops 22151168 | bytes 27262976 | tf_op jit(solution)/shard_map/convert.1
  690.4 0.0 copy-done.1
  690.4 10.8 %fusion.6 = bf16[896,3328]{0,1:T(8,128)(2,1)S(1)} fusion(bf16[1024,896]{1,0:T(8,128)(2,1)S(1)} %copy-done.1, bf16[1024,1664]{0,1:T(8,128)(2,1)S(1)} %get-tuple-element.7, bf16[1024,1664]{0,1:T(8,128)(2,1)S(1)} %get-tuple-element.6), kind=kOutput, calls=%fused_computation.11 | convolution fusion | flops 6123520000 | bytes 14614528 | tf_op jit(solution)/shard_map/dot_general | solution.py:31
  701.2 2.1 fusion.14
  703.3 5.4 copy.11
  708.6 3.5 copy.12
Async XLA Ops:
  7.2 40.8 %all-gather.2.cloned.1.call-start = ((), (), s32[]{:S(2)}) async-start(), calls=%async_computation.1 | async-start | bytes 1949696 | tf_op jit(solution)/shard_map/all_gather | solution.py:26
  7.9 673.6 %all-reduce.2.cloned.1.call-start = ((), (), s32[]{:S(2)}) async-start(), calls=%async_computation.2 | async-start | bytes 27262976 | tf_op jit(solution)/shard_map/psum | solution.py:28
  61.5 0.9 copy-start
  192.5 497.9 %copy-start.1 = (bf16[1024,896]{1,0:T(8,128)(2,1)S(1)}, bf16[1024,896]{1,0:T(8,128)(2,1)}, u32[]{:S(2)}) copy-start(bf16[1024,896]{1,0:T(8,128)(2,1)} %all-gather.2.cloned.1.call-done) | copy-start | bytes 5505028
Sparse Core Ops, SparseCore 0:
  9.8 38.1 all-gather.1
  61.7 619.7 all-reduce.1
